TPU v7x, 32 devices: a whole 2x2x4 slice. The times are simulated.
32 devices in a mesh: ctx: 2 (over y), fsdp: 4 (over z), rep: 4 (over x, core).
Axes of the slice: x: 2, y: 2, z: 4, core: 2. Of those that a mesh axis runs over, the one named last changes fastest.
Arguments:
- tokens: bfloat16 [16, 256, 2048], P(('fsdp', 'rep'), 'ctx'), may hold values from -6 to 6
- cotangent: bfloat16 [16, 256, 2048], P(('fsdp', 'rep'), 'ctx'), may hold values from -6 to 6
- lengths: int32 [16], P(('fsdp', 'rep')), may hold values from 64 to 256, as said below
- first_gain: bfloat16 [2048], P('fsdp'), may hold values from 0.25 to 1.75
- joint_matrix: bfloat16 [2048, 1920], P('fsdp'), may hold values from -0.125 to 0.125
- query_gain: bfloat16 [64], P('fsdp'), may hold values from 0.25 to 1.75
- key_gain: bfloat16 [64], P('fsdp'), may hold values from 0.25 to 1.75
- out_weight: bfloat16 [1280, 2048], P('fsdp'), may hold values from -2 to 2
- second_gain: bfloat16 [2048], P('fsdp'), may hold values from 0.25 to 1.75
- expand_weight: bfloat16 [2048, 10240], P('fsdp'), may hold values from -0.125 to 0.125
- contract_weight: bfloat16 [5120, 2048], P('fsdp'), may hold values from -0.078125 to 0.078125
Outputs:
- layer_output: bfloat16 [16, 256, 2048], P(('fsdp', 'rep'), 'ctx')
- input_gradient: float32 [16, 256, 2048], P(('fsdp', 'rep'), 'ctx')
- first_gradient: float32 [2048], P('fsdp')
- joint_gradient: float32 [2048, 1920], P('fsdp')
- query_gradient: float32 [64], P('fsdp')
- key_gradient: float32 [64], P('fsdp')
- out_gradient: float32 [1280, 2048], P('fsdp')
- second_gradient: float32 [2048], P('fsdp')
- expand_gradient: float32 [2048, 10240], P('fsdp')
- contract_gradient: float32 [5120, 2048], P('fsdp')
Inputs may be any that keep to these rules, and one draw needn't show every extreme that they name: `lengths`: valid positions count from each slot's start; some slot is full and some slot has 64.
All inputs are finite; a program needn't handle non-finite values.
Results may differ from a plain program's by a relative error of at most 0.012.
Values may be sent and summed in bfloat16 or wider, within the bound.
No kernel may reach another device: no remote copies, remote signals or barrier semaphores. Data moves between devices by JAX's collectives and lax.ppermute only.
A program may use at most 384 MiB of HBM per device.

v0:
```python
import math
import jax
import jax.numpy as jnp
from jax import lax
from jax.sharding import PartitionSpec as P

QUERY_HEADS = 20
KEY_VALUE_HEADS = 5
HEAD_SIZE = 64
FF = 5120
epsilon = 1e-06
masked_fill_value = -1e30


def tables(positions, width):
    steps = jnp.arange(width // 2, dtype=jnp.float32)
    rates = jnp.exp(steps * (-2.0 * math.log(10000.0) / width))
    angles = positions.astype(jnp.float32)[:, None] * rates[None, :]
    return (jnp.cos(angles)[:, None, :], jnp.sin(angles)[:, None, :])


def rotate(field, cosine_table, sine_table):
    half = field.shape[-1] // 2
    first, second = (field[..., :half], field[..., half:])
    return jnp.concatenate(
        [first * cosine_table - second * sine_table, second * cosine_table + first * sine_table],
        axis=-1,
    )


def reverse_rotation(upstream, cosine_table, sine_table):
    half = upstream.shape[-1] // 2
    first, second = (upstream[..., :half], upstream[..., half:])
    return jnp.concatenate(
        [first * cosine_table + second * sine_table, second * cosine_table - first * sine_table],
        axis=-1,
    )


def rms_parts(field):
    inverse = lax.rsqrt(jnp.mean(field * field, axis=-1, keepdims=True) + epsilon)
    return (field * inverse, inverse)


def rms_back(upstream, normed, inverse):
    return inverse * (upstream - normed * jnp.mean(upstream * normed, axis=-1, keepdims=True))


def cross_product(left, right):
    return lax.dot_general(
        left, right, (((0,), (0,)), ((), ())), preferred_element_type=jnp.float32
    )


def against(left, right):
    return lax.dot_general(
        left, right, (((1,), (1,)), ((), ())), preferred_element_type=jnp.float32
    )


def block_scores(grouped_query, pair_all, start, positions, slot_length_value, stretch_factor):
    key_span_width = KEY_VALUE_HEADS * HEAD_SIZE
    block_pairing = lax.dynamic_slice_in_dim(pair_all, start, stretch_factor, 0)
    key_rows = block_pairing[:, :key_span_width].reshape(stretch_factor, KEY_VALUE_HEADS, HEAD_SIZE)
    value_rows = block_pairing[:, key_span_width:].reshape(
        stretch_factor, KEY_VALUE_HEADS, HEAD_SIZE
    )
    scores = jnp.einsum(
        "qgrd,kgd->grqk", grouped_query, key_rows, preferred_element_type=jnp.float32
    ) * HEAD_SIZE ** (-0.5)
    key_pos = start + jnp.arange(stretch_factor, dtype=jnp.int32)
    allowed = (key_pos[None, :] <= positions[:, None]) & (key_pos[None, :] < slot_length_value)
    scores = jnp.where(allowed, scores, masked_fill_value)
    return (scores, allowed, key_rows, value_rows)


def shards(
    tokens,
    cotangent,
    lengths,
    first_gain,
    joint_matrix,
    query_gain,
    key_gain,
    out_weight,
    second_gain,
    expand_weight,
    contract_weight,
):
    stretch_factor = tokens.shape[1]
    place = lax.axis_index("ctx")
    span = stretch_factor * lax.axis_size("ctx")
    slot_length_value = lengths[0]
    positions = place * stretch_factor + jnp.arange(stretch_factor, dtype=jnp.int32)
    valid = (positions < slot_length_value).astype(jnp.float32)[:, None]
    context_block_count = jnp.minimum(place, (slot_length_value - 1) // stretch_factor) + 1
    query_span_width = QUERY_HEADS * HEAD_SIZE
    key_span_width = KEY_VALUE_HEADS * HEAD_SIZE
    head_group = QUERY_HEADS // KEY_VALUE_HEADS
    scale = HEAD_SIZE ** (-0.5)
    gain_one, joint_full, query_scale, key_scale, out_full = (
        lax.all_gather(first_gain, "fsdp", axis=0, tiled=True),
        lax.all_gather(joint_matrix, "fsdp", axis=0, tiled=True),
        lax.all_gather(query_gain, "fsdp", axis=0, tiled=True),
        lax.all_gather(key_gain, "fsdp", axis=0, tiled=True),
        lax.all_gather(out_weight, "fsdp", axis=0, tiled=True),
    )
    rows = tokens[0].astype(jnp.float32)
    normed_one, inverse_one = rms_parts(rows)
    entry_one = (normed_one * gain_one.astype(jnp.float32)).astype(jnp.bfloat16)
    joint_projection = jnp.dot(entry_one, joint_full, preferred_element_type=jnp.float32)
    query_raw = joint_projection[:, :query_span_width].reshape(
        stretch_factor, QUERY_HEADS, HEAD_SIZE
    )
    unnormed_key = joint_projection[
        :, query_span_width : query_span_width + key_span_width
    ].reshape(stretch_factor, KEY_VALUE_HEADS, HEAD_SIZE)
    value_part = joint_projection[:, query_span_width + key_span_width :]
    cosine_table, sine_table = tables(positions, HEAD_SIZE)
    query_normed, query_inverse = rms_parts(query_raw)
    rotated_query = rotate(
        query_normed * query_scale.astype(jnp.float32), cosine_table, sine_table
    ).astype(jnp.bfloat16)
    key_normed, key_inverse = rms_parts(unnormed_key)
    key_rot = rotate(key_normed * key_scale.astype(jnp.float32), cosine_table, sine_table).astype(
        jnp.bfloat16
    )
    local_pair = jnp.concatenate(
        [key_rot.reshape(stretch_factor, key_span_width), value_part.astype(jnp.bfloat16)], axis=1
    )
    pair_all = lax.all_gather(local_pair, "ctx", axis=0, tiled=True)
    grouped_query = rotated_query.reshape(stretch_factor, KEY_VALUE_HEADS, head_group, HEAD_SIZE)

    def largest_step(index, carry):
        running, total = carry
        scores, allowed, key_rows, value_rows = block_scores(
            grouped_query,
            pair_all,
            index * stretch_factor,
            positions,
            slot_length_value,
            stretch_factor,
        )
        newer = jnp.maximum(running, jnp.max(scores, axis=-1))
        total = total * jnp.exp(running - newer) + jnp.sum(
            jnp.exp(scores - newer[..., None]), axis=-1
        )
        return (newer, total)

    largest_start = jnp.full(
        (KEY_VALUE_HEADS, head_group, stretch_factor), masked_fill_value, jnp.float32
    )
    running, total = lax.fori_loop(
        0,
        context_block_count,
        largest_step,
        (largest_start, jnp.zeros((KEY_VALUE_HEADS, head_group, stretch_factor), jnp.float32)),
    )
    log_total = running + jnp.log(total)

    def value_step(index, carry):
        rounded, exact = carry
        scores, allowed, key_rows, value_rows = block_scores(
            grouped_query,
            pair_all,
            index * stretch_factor,
            positions,
            slot_length_value,
            stretch_factor,
        )
        shares = jnp.where(allowed, jnp.exp(scores - log_total[..., None]), 0.0)
        rounded = rounded + jnp.einsum(
            "grqk,kgd->qgrd",
            shares.astype(jnp.bfloat16),
            value_rows,
            preferred_element_type=jnp.float32,
        )
        exact = exact + jnp.einsum(
            "grqk,kgd->qgrd",
            shares,
            value_rows.astype(jnp.float32),
            precision=lax.Precision.HIGHEST,
        )
        return (rounded, exact)

    blank_group = jnp.zeros((stretch_factor, KEY_VALUE_HEADS, head_group, HEAD_SIZE), jnp.float32)
    rounded, exact = lax.fori_loop(0, context_block_count, value_step, (blank_group, blank_group))
    mixed_output = rounded.reshape(stretch_factor, query_span_width).astype(jnp.bfloat16)
    hidden = rows + jnp.dot(mixed_output, out_full, preferred_element_type=jnp.float32)
    gain_two, expand_full, contract_full = (
        lax.all_gather(second_gain, "fsdp", axis=0, tiled=True),
        lax.all_gather(expand_weight, "fsdp", axis=0, tiled=True),
        lax.all_gather(contract_weight, "fsdp", axis=0, tiled=True),
    )
    normed_two, inverse_two = rms_parts(hidden)
    entry_two = (normed_two * gain_two.astype(jnp.float32)).astype(jnp.bfloat16)
    expanded = jnp.dot(entry_two, expand_full, preferred_element_type=jnp.float32)
    gate = expanded[:, :FF]
    upward = expanded[:, FF:]
    sigma = jax.nn.sigmoid(gate)
    activated = gate * sigma
    product = (activated * upward).astype(jnp.bfloat16)
    branch_two = jnp.dot(product, contract_full, preferred_element_type=jnp.float32)
    layer_output = ((hidden + branch_two) * valid).astype(jnp.bfloat16)
    gain_two, expand_full, contract_full = (
        lax.all_gather(second_gain, "fsdp", axis=0, tiled=True),
        lax.all_gather(expand_weight, "fsdp", axis=0, tiled=True),
        lax.all_gather(contract_weight, "fsdp", axis=0, tiled=True),
    )
    upstream = cotangent[0].astype(jnp.float32) * valid
    upstream_b = upstream.astype(jnp.bfloat16)
    contract_grad = cross_product(product, upstream_b)
    back_product = against(upstream_b, contract_full)
    grad_gate = back_product * upward * sigma * (1.0 + gate * (1.0 - sigma))
    grad_upward = back_product * activated
    grad_expanded = jnp.concatenate([grad_gate, grad_upward], axis=1).astype(jnp.bfloat16)
    expand_grad = cross_product(entry_two, grad_expanded)
    back_entry_two = against(grad_expanded, expand_full)
    second_grad = jnp.sum(back_entry_two * normed_two, axis=0)
    back_hidden = upstream + rms_back(
        back_entry_two * gain_two.astype(jnp.float32), normed_two, inverse_two
    )
    second_owned, expand_owned, contract_owned = (
        lax.psum_scatter(second_grad, "fsdp", scatter_dimension=0, tiled=True),
        lax.psum_scatter(expand_grad, "fsdp", scatter_dimension=0, tiled=True),
        lax.psum_scatter(contract_grad, "fsdp", scatter_dimension=0, tiled=True),
    )
    gain_one, joint_full, query_scale, key_scale, out_full = (
        lax.all_gather(first_gain, "fsdp", axis=0, tiled=True),
        lax.all_gather(joint_matrix, "fsdp", axis=0, tiled=True),
        lax.all_gather(query_gain, "fsdp", axis=0, tiled=True),
        lax.all_gather(key_gain, "fsdp", axis=0, tiled=True),
        lax.all_gather(out_weight, "fsdp", axis=0, tiled=True),
    )
    back_hidden_b = back_hidden.astype(jnp.bfloat16)
    out_grad = cross_product(mixed_output, back_hidden_b)
    mixed_backward = against(back_hidden_b, out_full).astype(jnp.bfloat16)
    group_backward = mixed_backward.reshape(stretch_factor, KEY_VALUE_HEADS, head_group, HEAD_SIZE)
    offset = jnp.transpose(jnp.sum(group_backward.astype(jnp.float32) * exact, axis=-1), (1, 2, 0))
    pair_all = lax.all_gather(local_pair, "ctx", axis=0, tiled=True)

    def grad_step(index, carry):
        grad_query, pair_grads = carry
        start = index * stretch_factor
        scores, allowed, key_rows, value_rows = block_scores(
            grouped_query, pair_all, start, positions, slot_length_value, stretch_factor
        )
        shares = jnp.where(allowed, jnp.exp(scores - log_total[..., None]), 0.0)
        back_shares = jnp.einsum(
            "qgrd,kgd->grqk", group_backward, value_rows, preferred_element_type=jnp.float32
        )
        back_scores = (shares * (back_shares - offset[..., None])).astype(jnp.bfloat16)
        grad_query = grad_query + jnp.einsum(
            "grqk,kgd->qgrd", back_scores, key_rows, preferred_element_type=jnp.float32
        )
        grad_keys = (
            jnp.einsum(
                "grqk,qgrd->kgd", back_scores, grouped_query, preferred_element_type=jnp.float32
            )
            * scale
        )
        grad_values = jnp.einsum(
            "grqk,qgrd->kgd",
            shares.astype(jnp.bfloat16),
            group_backward,
            preferred_element_type=jnp.float32,
        )
        block_grad = jnp.concatenate(
            [
                grad_keys.reshape(stretch_factor, key_span_width),
                grad_values.reshape(stretch_factor, key_span_width),
            ],
            axis=1,
        )
        pair_grads = lax.dynamic_update_slice_in_dim(pair_grads, block_grad, start, 0)
        return (grad_query, pair_grads)

    grad_query, pair_grads = lax.fori_loop(
        0,
        context_block_count,
        grad_step,
        (blank_group, jnp.zeros((span, 2 * key_span_width), jnp.float32)),
    )
    local_pairing = lax.psum_scatter(pair_grads, "ctx", scatter_dimension=0, tiled=True)
    back_query_rot = reverse_rotation(
        grad_query.reshape(stretch_factor, QUERY_HEADS, HEAD_SIZE) * scale, cosine_table, sine_table
    )
    query_gain_grad = jnp.sum(back_query_rot * query_normed, axis=(0, 1))
    grad_query_raw = rms_back(
        back_query_rot * query_scale.astype(jnp.float32), query_normed, query_inverse
    )
    rotated_key_backward = reverse_rotation(
        local_pairing[:, :key_span_width].reshape(stretch_factor, KEY_VALUE_HEADS, HEAD_SIZE),
        cosine_table,
        sine_table,
    )
    key_gain_grad = jnp.sum(rotated_key_backward * key_normed, axis=(0, 1))
    grad_key_raw = rms_back(
        rotated_key_backward * key_scale.astype(jnp.float32), key_normed, key_inverse
    )
    grad_joint = jnp.concatenate(
        [
            grad_query_raw.reshape(stretch_factor, query_span_width),
            grad_key_raw.reshape(stretch_factor, key_span_width),
            local_pairing[:, key_span_width:],
        ],
        axis=1,
    ).astype(jnp.bfloat16)
    joint_grad = cross_product(entry_one, grad_joint)
    back_entry_one = against(grad_joint, joint_full)
    first_grad = jnp.sum(back_entry_one * normed_one, axis=0)
    input_gradient = back_hidden + rms_back(
        back_entry_one * gain_one.astype(jnp.float32), normed_one, inverse_one
    )
    first_owned, joint_owned, query_owned, key_owned, out_owned = (
        lax.psum_scatter(first_grad, "fsdp", scatter_dimension=0, tiled=True),
        lax.psum_scatter(joint_grad, "fsdp", scatter_dimension=0, tiled=True),
        lax.psum_scatter(query_gain_grad, "fsdp", scatter_dimension=0, tiled=True),
        lax.psum_scatter(key_gain_grad, "fsdp", scatter_dimension=0, tiled=True),
        lax.psum_scatter(out_grad, "fsdp", scatter_dimension=0, tiled=True),
    )
    summed = lax.psum(
        (
            first_owned,
            joint_owned,
            query_owned,
            key_owned,
            out_owned,
            second_owned,
            expand_owned,
            contract_owned,
        ),
        ("ctx", "rep"),
    )
    return (layer_output[None], input_gradient[None]) + tuple(summed)


def solution(mesh):
    return jax.shard_map(
        shards,
        mesh=mesh,
        in_specs=(
            P(("fsdp", "rep"), "ctx", None),
            P(("fsdp", "rep"), "ctx", None),
            P(("fsdp", "rep")),
            P("fsdp"),
            P("fsdp", None),
            P("fsdp"),
            P("fsdp"),
            P("fsdp", None),
            P("fsdp"),
            P("fsdp", None),
            P("fsdp", None),
        ),
        out_specs=(
            P(("fsdp", "rep"), "ctx", None),
            P(("fsdp", "rep"), "ctx", None),
            P("fsdp"),
            P("fsdp", None),
            P("fsdp"),
            P("fsdp"),
            P("fsdp", None),
            P("fsdp"),
            P("fsdp", None),
            P("fsdp", None),
        ),
        check_vma=False,
    )
```

profile of v0, /device:TPU:0, one launch (start us, length us, event | category | flops | bytes accessed | tf_op | source)
XLA Modules:
  0.0 4372.1 jit_solution(18229859901072036340)
XLA Ops:
  10.8 13.5 all-gather
  26.1 12.9 all-reduce.10
  39.1 13.1 all-gather.1
  52.7 101.0 %all-gather.7.cloned.1.call-done = bf16[2048,1920]{1,0:T(8,128)(2,1)} async-done(((bf16[512,1920]{1,0:T(8,128)(2,1)}), bf16[2048,1920]{1,0:T(8,128)(2,1)}) %all-gather.7.cloned.1.call-update) | async-done | bytes 7864336 | tf_op jit(solution)/shard_map/all_gather | solution.py:103
  153.7 4.5 fusion.59
  160.3 6.8 all_gather.39
  169.5 2.4 while.39
  172.6 4.4 while.40
  174.3 1.2 fusion.135
  177.0 74.6 %all-gather.9.cloned.1.call-done = bf16[1280,2048]{1,0:T(8,128)(2,1)} async-done(((bf16[320,2048]{1,0:T(8,128)(2,1)}), bf16[1280,2048]{1,0:T(8,128)(2,1)}) %all-gather.9.cloned.1.call-update) | async-done | bytes 5242896 | tf_op jit(solution)/shard_map/all_gather | solution.py:106
  251.7 3.4 multiply_reduce_fusion.2
  255.2 696.3 %all-gather.11.cloned.1.call-done = bf16[2048,10240]{1,0:T(8,128)(2,1)} async-done(((bf16[512,10240]{1,0:T(8,128)(2,1)}), bf16[2048,10240]{1,0:T(8,128)(2,1)}) %all-gather.11.cloned.1.call-update) | async-done | bytes 41943056 | tf_op jit(solution)/shard_map/all_gather | solution.py:192
  951.5 21.9 fusion.64
  973.4 334.6 %all-gather.13.cloned.1.call-done = bf16[5120,2048]{1,0:T(8,128)(2,1)} async-done(((bf16[1280,2048]{1,0:T(8,128)(2,1)}), bf16[5120,2048]{1,0:T(8,128)(2,1)}) %all-gather.13.cloned.1.call-update) | async-done | bytes 20971536 | tf_op jit(solution)/shard_map/all_gather | solution.py:193
  1308.0 13.6 multiply_convert_fusion.1
  1321.6 20.5 multiply_reduce_fusion
  1342.5 1.0 copy-done.1
  1343.5 4.3 convolution_convert_fusion
  1349.7 6.1 while.41
  1351.6 1.2 fusion.149
  1352.8 1.1 fusion.150
  1355.9 6.9 fusion.48
  1365.1 2.1 copy.123
  1367.4 1.0 pad_maximum_fusion.4
  1368.4 2.2 copy.120
  1370.7 1.1 copy.122
  1371.8 3.0 multiply_reduce_fusion.3
  1374.8 1.8 reduce-scatter.8.cloned.1.call-done
  1378.6 1.0 slice.125
  1379.8 8.5 fusion.57
  1388.4 1.2 copy-done.5
  1389.6 17.5 fusion.51
  1407.3 30.9 fusion.32
  1438.3 119.1 %reduce-scatter.12.cloned.1.call-done = f32[320,2048]{1,0:T(8,128)} async-done(((f32[1280,2048]{1,0:T(8,128)}), f32[320,2048]{1,0:T(8,128)}) %reduce-scatter.12.cloned.1.call-update) | async-done | bytes 2621456 | tf_op jit(solution)/shard_map/reduce_scatter | solution.py:320
  1557.5 266.8 %reduce-scatter.10.cloned.1.call-done = f32[512,1920]{1,0:T(8,128)} async-done(((f32[2048,1920]{1,0:T(8,128)}), f32[512,1920]{1,0:T(8,128)}) %reduce-scatter.10.cloned.1.call-update) | async-done | bytes 3932176 | tf_op jit(solution)/shard_map/reduce_scatter | solution.py:317
  1824.2 689.9 %reduce-scatter.14.cloned.1.call-done = f32[1280,2048]{1,0:T(8,128)} async-done(((f32[5120,2048]{1,0:T(8,128)}), f32[1280,2048]{1,0:T(8,128)}) %reduce-scatter.14.cloned.1.call-update) | async-done | bytes 10485776 | tf_op jit(solution)/shard_map/reduce_scatter | solution.py:226
  2514.1 1368.5 %reduce-scatter.16.cloned.1.call-done = f32[512,10240]{1,0:T(8,128)} async-done(((f32[2048,10240]{1,0:T(8,128)}), f32[512,10240]{1,0:T(8,128)}) %reduce-scatter.16.cloned.1.call-update) | async-done | bytes 20971536
  3884.6 1.2 reduce_sum.152
  3885.8 10.7 fusion.31
  3896.8 6.1 fusion.44
  3902.9 19.1 all-reduce.9
  3922.2 13.2 all-reduce.7
  3935.5 1.3 fusion.43
  3936.8 400.2 %all-reduce.13.cloned.1.call-done = (f32[512,1920]{1,0:T(8,128)}, f32[320,2048]{1,0:T(8,128)}, f32[512,10240]{1,0:T(8,128)}, f32[1280,2048]{1,0:T(8,128)}) async-done(((f32[512,1920]{1,0:T(8,128)}, f32[320,2048]{1,0:T(8,128)}, f32[512,10240]{1,0:T(8,128)}, f32[1280,2048]{1,0:T(8,128)}), (f32[512,1920]{1,0:T(8,128)}, f32[320,2048]{1,0:T(8,128)}, f32[512,10240]{1,0:T(8,128)}, ...) | async-done | bytes 38010896 | tf_op jit(solution)/shard_map/psum | solution.py:322
  4337.0 4.4 copy.197
  4341.5 1.5 copy.198
  4343.0 18.0 copy.199
  4361.0 4.1 copy.200
  (214 shorter events, 26.4 us)
Async XLA Ops:
  7.2 146.6 %all-gather.7.cloned.1.call-start = ((), (), s32[]{:S(2)}) async-start(), calls=%async_computation.5 | async-start | bytes 9830400 | tf_op jit(solution)/shard_map/all_gather | solution.py:103
  7.9 243.8 %all-gather.9.cloned.1.call-start = ((), (), s32[]{:S(2)}) async-start(), calls=%async_computation.6 | async-start | bytes 6553600 | tf_op jit(solution)/shard_map/all_gather | solution.py:106
  8.7 942.8 %all-gather.11.cloned.1.call-start = ((), (), s32[]{:S(2)}) async-start(), calls=%async_computation.7 | async-start | bytes 52428800 | tf_op jit(solution)/shard_map/all_gather | solution.py:192
  9.4 1.4 copy-start.37
  9.4 15.0 copy-start.35
  9.4 16.2 copy-start.43
  9.4 16.5 copy-start.44
  9.4 29.7 copy-start.38
  9.4 42.9 copy-start
  9.5 1298.5 %all-gather.13.cloned.1.call-start = ((), (), s32[]{:S(2)}) async-start(), calls=%async_computation.8 | async-start | bytes 26214400 | tf_op jit(solution)/shard_map/all_gather | solution.py:193
  10.0 1366.5 %reduce-scatter.8.cloned.1.call-start = ((), (), s32[]{:S(2)}) async-start(), calls=%async_computation.9 | async-start | bytes 983040 | tf_op jit(solution)/shard_map/reduce_scatter | solution.py:284
  39.1 13.2 copy-start.39
  39.1 119.2 %copy-start.41 = (bf16[64]{0:T(256)(128)(2,1)}, bf16[64]{0:T(256)(128)(2,1)S(1)}, u32[]{:S(2)}) copy-start(bf16[64]{0:T(256)(128)(2,1)S(1)} %get-tuple-element.449) | copy-start | bytes 388
  39.1 120.4 %copy-start.31 = (f32[64]{0:T(128)}, f32[64]{0:T(128)S(1)}, u32[]{:S(2)}) copy-start(f32[64]{0:T(128)S(1)} %convert_element_type.96) | copy-start | bytes 772
  39.1 129.2 %copy-start.33 = (f32[64]{0:T(128)}, f32[64]{0:T(128)S(1)}, u32[]{:S(2)}) copy-start(f32[64]{0:T(128)S(1)} %convert_element_type.99) | copy-start | bytes 772
  52.3 1289.8 %copy-start.30 = (f32[128]{0:T(128)}, f32[128]{0:T(128)S(1)}, u32[]{:S(2)}) copy-start(f32[128]{0:T(128)S(1)} %compare_convert_fusion) | copy-start | bytes 1540
  52.5 105.7 %copy-start.26 = (f32[128]{0:T(128)}, f32[128]{0:T(128)S(1)}, u32[]{:S(2)}) copy-start(f32[128]{0:T(128)S(1)} %add_rsqrt_fusion.3) | copy-start | bytes 1540
  52.7 116.6 %copy-start.15 = (f32[128,32]{0,1:T(8,128)}, f32[128,32]{0,1:T(8,128)S(1)}, u32[]{:S(2)}) copy-start(f32[128,32]{0,1:T(8,128)S(1)} %get-tuple-element.481) | copy-start | bytes 49156
  52.7 116.6 %copy-start.17 = (f32[128,32]{0,1:T(8,128)}, f32[128,32]{0,1:T(8,128)S(1)}, u32[]{:S(2)}) copy-start(f32[128,32]{0,1:T(8,128)S(1)} %get-tuple-element.482) | copy-start | bytes 49156
  159.4 7.7 copy-start.8
  177.0 78.1 %copy-start.10 = (bf16[128,5,4,64]{0,3,2,1:T(8,128)(2,1)}, bf16[128,5,4,64]{0,3,2,1:T(8,128)(2,1)S(1)}, u32[]{:S(2)}) copy-start(bf16[128,5,4,64]{0,3,2,1:T(8,128)(2,1)S(1)} %convert_element_type.100) | copy-start | bytes 983044
  255.2 1086.9 %copy-start.23 = (f32[128]{0:T(128)}, f32[128]{0:T(128)S(1)}, u32[]{:S(2)}) copy-start(f32[128]{0:T(128)S(1)} %add_rsqrt_fusion.2) | copy-start | bytes 1540
  951.5 356.5 %copy-start.12 = (bf16[1,128,2048]{2,1,0:T(8,128)(2,1)S(1)}, bf16[1,128,2048]{2,1,0:T(8,128)(2,1)}, u32[]{:S(2)}) copy-start(bf16[1,128,2048]{2,1,0:T(8,128)(2,1)} %param.18) | copy-start | bytes 1572868
  1355.9 201.6 %reduce-scatter.12.cloned.1.call-start = ((), (), s32[]{:S(2)}) async-start(), calls=%async_computation.11 | async-start | bytes 13107200 | tf_op jit(solution)/shard_map/reduce_scatter | solution.py:320
  1362.9 4.4 copy-start.16
  1362.9 4.4 copy-start.18
  1362.9 4.5 copy-start.4
  1362.9 4.5 copy-start.34
  1362.9 461.3 %reduce-scatter.10.cloned.1.call-start = ((), (), s32[]{:S(2)}) async-start(), calls=%async_computation.10 | async-start | bytes 19660800 | tf_op jit(solution)/shard_map/reduce_scatter | solution.py:317
  1367.4 4.3 copy-start.7
  1370.7 6.9 copy-start.9
  1371.8 5.9 copy-start.22
  1371.8 5.9 copy-start.32
  1371.8 6.0 copy-start.29
  1371.8 8.0 copy-start.27
  1374.8 4.9 copy-start.13
  1388.3 1125.8 %reduce-scatter.14.cloned.1.call-start = ((), (), s32[]{:S(2)}) async-start(), calls=%async_computation.12 | async-start | bytes 52428800 | tf_op jit(solution)/shard_map/reduce_scatter | solution.py:226
  1407.1 2475.5 %reduce-scatter.16.cloned.1.call-start = ((), (), s32[]{:S(2)}) async-start(), calls=%async_computation.13 | async-start | bytes 104857600
  1438.3 2898.8 %all-reduce.13.cloned.1.call-start = ((), (), s32[]{:S(2)}) async-start(), calls=%async_computation.14 | async-start | bytes 76021760 | tf_op jit(solution)/shard_map/psum | solution.py:322
  3885.8 10.7 copy-start.14
  3885.8 10.9 copy-start.28
  3896.8 6.1 copy-start.24
  3896.8 6.1 copy-start.36
  3896.8 38.7 copy-start.2
  4337.0 4.4 copy-start.11
  4341.5 19.5 slice-start
  4343.0 18.0 slice-start.1
  4343.0 18.0 slice-start.2
  (10 other events, 9.7 us)
Sparse Core Ops, SparseCore 0:
  9.6 144.1 all-gather.6
  155.3 96.3 all-gather.8
  253.3 698.1 all-gather.10
  952.9 355.0 all-gather.12
  1356.0 20.4 reduce-scatter.7
  1379.4 177.9 reduce-scatter.11
  1560.5 263.6 reduce-scatter.9
  1826.7 687.3 reduce-scatter.13
  2516.5 1366.0 reduce-scatter.15
  3887.2 449.7 all-reduce.12
where the time goes:
time: 4380 us; the launch traced here: 4370 us
  waiting for transfers between devices  4060 us (93%)
  matrix products  155 us (4%)
  blocking collectives  78.7 us (2%)
  local copies, waits for them, and re-layouts  51 us (1%)
    unnamed x11, waiting for transfers between devices  1370 us
    all_gather x1, waiting for transfers between devices, shards(): lax.all_gather(expand_weight, 'fsdp', axis=0, tiled=True)  696 us
    reduce_scatter x1, waiting for transfers between devices, shards(): lax.psum_scatter(contract_grad, 'fsdp', scatter_dimension=0, tiled=True)  690 us
    psum x1, waiting for transfers between devices, shards(): lax.psum((first_owned, joint_owned, query_owned, key_owned, out_owned, se...  400 us
    all_gather x1, waiting for transfers between devices, shards(): lax.all_gather(contract_weight, 'fsdp', axis=0, tiled=True)  335 us
    reduce_scatter x1, waiting for transfers between devices, shards(): lax.psum_scatter(joint_grad, 'fsdp', scatter_dimension=0, tiled=True)  267 us
    reduce_scatter x1, waiting for transfers between devices, shards(): lax.psum_scatter(out_grad, 'fsdp', scatter_dimension=0, tiled=True)  119 us
    all_gather x1, waiting for transfers between devices, shards(): lax.all_gather(joint_matrix, 'fsdp', axis=0, tiled=True)  101 us
  transfers between devices with their start and end apart: 10, of which 10 were waited for; matrix products, arithmetic and copies ran while one was open for 3% of the time, Pallas kernels for 0%

commit v1 on v0

--- a/solution.py
+++ b/solution.py
@@ -10,6 +10,32 @@
 FF = 5120
 epsilon = 1e-06
 masked_fill_value = -1e30
+
+
+def cut_zone(z, group_axis):
+    r1, val2, long_array = (lax.axis_size(group_axis), lax.axis_index(group_axis), z.shape[0])
+    q_next = lax.dynamic_update_slice_in_dim(
+        jnp.zeros([hop_no * r1 if t == 0 else hop_no for t, hop_no in enumerate(z.shape)], z.dtype),
+        z,
+        val2 * long_array,
+        axis=0,
+    )
+    parts_out = x_new = z
+    for to_i in range(1, r1 // 2 + 1):
+        parts_out = lax.ppermute(
+            parts_out, group_axis, list(map(lambda t: (t, (t + 1) % r1), range(r1)))
+        )
+        q_next = lax.dynamic_update_slice_in_dim(
+            q_next, parts_out, (val2 - to_i) % r1 * long_array, axis=0
+        )
+        if 2 * to_i < r1:
+            x_new = lax.ppermute(
+                x_new, group_axis, list(map(lambda t: (t, (t - 1) % r1), range(r1)))
+            )
+            q_next = lax.dynamic_update_slice_in_dim(
+                q_next, x_new, (val2 + to_i) % r1 * long_array, axis=0
+            )
+    return q_next
 
 
 def tables(positions, width):
@@ -190,7 +216,7 @@
     gain_two, expand_full, contract_full = (
         lax.all_gather(second_gain, "fsdp", axis=0, tiled=True),
         lax.all_gather(expand_weight, "fsdp", axis=0, tiled=True),
-        lax.all_gather(contract_weight, "fsdp", axis=0, tiled=True),
+        cut_zone(contract_weight, "fsdp"),
     )
     normed_two, inverse_two = rms_parts(hidden)
     entry_two = (normed_two * gain_two.astype(jnp.float32)).astype(jnp.bfloat16)

time: 4380 us -> 4380 us (level)
  waiting for transfers between devices: 4060 us -> 3910 us
  starting transfers between devices: 0.61 us -> 116 us
    psum x1, waiting for transfers between devices: 400 us -> 54.2 us  [shards(): lax.psum((first_owned, joint_owned, query_owned, key_owned, out_owned, se...]
    ppermute x0 -> x3, waiting for transfers between devices: none -> 202 us  [the longest x2 202 us: cut_zone(): lax.ppermute(parts_out, group_axis, list(map(lambda t: (t, (t + 1) % r1),...]
    ppermute x0 -> x3, starting transfers between devices: none -> 115 us  [the longest x2 111 us: cut_zone(): lax.ppermute(parts_out, group_axis, list(map(lambda t: (t, (t + 1) % r1),...]
  transfers between devices with their start and end apart: 10 -> 13, of which waited for: 10 -> 12; matrix products, arithmetic and copies ran while one was open for 3% -> 4% of each run, Pallas kernels for 0% -> 0%
where the time goes in v1:
time: 4380 us; the launch traced here: 4370 us
  waiting for transfers between devices  3910 us (89%)
  matrix products  156 us (4%)
  starting transfers between devices  116 us (3%)
  local copies, waits for them, and re-layouts  81.6 us (2%)
  blocking collectives  76.7 us (2%)
    unnamed x11, waiting for transfers between devices  1370 us
    all_gather x1, waiting for transfers between devices, shards(): lax.all_gather(expand_weight, 'fsdp', axis=0, tiled=True)  696 us
    reduce_scatter x1, waiting for transfers between devices, shards(): lax.psum_scatter(contract_grad, 'fsdp', scatter_dimension=0, tiled=True)  690 us
    all_gather x1, waiting for transfers between devices, shards(): lax.all_gather(contract_weight, 'fsdp', axis=0, tiled=True)  335 us
    reduce_scatter x1, waiting for transfers between devices, shards(): lax.psum_scatter(joint_grad, 'fsdp', scatter_dimension=0, tiled=True)  267 us
    ppermute x2, waiting for transfers between devices, cut_zone(): lax.ppermute(parts_out, group_axis, list(map(lambda t: (t, (t + 1) % r1),...  202 us
    reduce_scatter x1, waiting for transfers between devices, shards(): lax.psum_scatter(out_grad, 'fsdp', scatter_dimension=0, tiled=True)  119 us
    ppermute x2, starting transfers between devices, cut_zone(): lax.ppermute(parts_out, group_axis, list(map(lambda t: (t, (t + 1) % r1),...  111 us
  transfers between devices with their start and end apart: 13, of which 12 were waited for; matrix products, arithmetic and copies ran while one was open for 4% of the time, Pallas kernels for 0%

profile of v1, /device:TPU:0, one launch (start us, length us, event | category | flops | bytes accessed | tf_op | source)
XLA Modules:
  0.0 4372.1 jit_solution(14978836218572980852)
XLA Ops:
  10.8 13.5 all-gather
  26.1 12.9 all-reduce.10
  39.1 13.1 all-gather.1
  52.7 101.0 %all-gather.7.cloned.1.call-done = bf16[2048,1920]{1,0:T(8,128)(2,1)} async-done(((bf16[512,1920]{1,0:T(8,128)(2,1)}), bf16[2048,1920]{1,0:T(8,128)(2,1)}) %all-gather.7.cloned.1.call-update) | async-done | bytes 7864336 | tf_op jit(solution)/shard_map/all_gather | solution.py:129
  153.7 4.5 fusion.59
  159.0 6.8 all_gather.38
  167.9 2.4 while.39
  171.0 4.4 while.40
  175.5 76.2 %all-gather.9.cloned.1.call-done = bf16[1280,2048]{1,0:T(8,128)(2,1)} async-done(((bf16[320,2048]{1,0:T(8,128)(2,1)}), bf16[1280,2048]{1,0:T(8,128)(2,1)}) %all-gather.9.cloned.1.call-update) | async-done | bytes 5242896 | tf_op jit(solution)/shard_map/all_gather | solution.py:132
  251.7 3.4 multiply_reduce_fusion.2
  255.2 696.3 %all-gather.11.cloned.1.call-done = bf16[2048,10240]{1,0:T(8,128)(2,1)} async-done(((bf16[512,10240]{1,0:T(8,128)(2,1)}), bf16[2048,10240]{1,0:T(8,128)(2,1)}) %all-gather.11.cloned.1.call-update) | async-done | bytes 41943056 | tf_op jit(solution)/shard_map/all_gather | solution.py:218
  951.5 21.9 fusion.64
  973.4 334.6 %all-gather.13.cloned.1.call-done = bf16[5120,2048]{1,0:T(8,128)(2,1)} async-done(((bf16[1280,2048]{1,0:T(8,128)(2,1)}), bf16[5120,2048]{1,0:T(8,128)(2,1)}) %all-gather.13.cloned.1.call-update) | async-done | bytes 20971536 | tf_op jit(solution)/shard_map/all_gather | solution.py:234
  1308.0 13.6 multiply_convert_fusion.1
  1321.6 20.5 multiply_reduce_fusion
  1343.5 4.3 convolution_convert_fusion
  1349.7 6.1 while.41
  1355.9 6.9 fusion.48
  1365.6 2.3 copy.123
  1369.1 2.3 copy.120
  1372.6 1.7 multiply_reduce_fusion.3
  1374.3 2.2 reduce-scatter.8.cloned.1.call-done
  1379.9 8.5 fusion.57
  1389.7 17.5 fusion.51
  1407.8 30.9 fusion.32
  1438.8 118.7 %reduce-scatter.12.cloned.1.call-done = f32[320,2048]{1,0:T(8,128)} async-done(((f32[1280,2048]{1,0:T(8,128)}), f32[320,2048]{1,0:T(8,128)}) %reduce-scatter.12.cloned.1.call-update) | async-done | bytes 2621456 | tf_op jit(solution)/shard_map/reduce_scatter | solution.py:346
  1557.4 266.8 %reduce-scatter.10.cloned.1.call-done = f32[512,1920]{1,0:T(8,128)} async-done(((f32[2048,1920]{1,0:T(8,128)}), f32[512,1920]{1,0:T(8,128)}) %reduce-scatter.10.cloned.1.call-update) | async-done | bytes 3932176 | tf_op jit(solution)/shard_map/reduce_scatter | solution.py:343
  1824.2 689.9 %reduce-scatter.14.cloned.1.call-done = f32[1280,2048]{1,0:T(8,128)} async-done(((f32[5120,2048]{1,0:T(8,128)}), f32[1280,2048]{1,0:T(8,128)}) %reduce-scatter.14.cloned.1.call-update) | async-done | bytes 10485776 | tf_op jit(solution)/shard_map/reduce_scatter | solution.py:252
  2514.1 1368.5 %reduce-scatter.16.cloned.1.call-done = f32[512,10240]{1,0:T(8,128)} async-done(((f32[2048,10240]{1,0:T(8,128)}), f32[512,10240]{1,0:T(8,128)}) %reduce-scatter.16.cloned.1.call-update) | async-done | bytes 20971536
  3882.6 3.8 collective-permute-start.1
  3886.4 114.2 %collective-permute-done = bf16[1280,2048]{1,0:T(8,128)(2,1)} collective-permute-done((bf16[1280,2048]{1,0:T(8,128)(2,1)}, bf16[1280,2048]{1,0:T(8,128)(2,1)}, u32[]{:S(2)}, u32[]{:S(2)}) %collective-permute-start) | collective-permute-done | bytes 5242912 | tf_op jit(solution)/shard_map/ppermute | solution.py:25
  4000.7 111.4 %collective-permute-start.2 = (bf16[1280,2048]{1,0:T(8,128)(2,1)}, bf16[1280,2048]{1,0:T(8,128)(2,1)}, u32[]{:S(2)}, u32[]{:S(2)}) collective-permute-start(bf16[1280,2048]{1,0:T(8,128)(2,1)} %collective-permute-done), channel_id=1, source_target_pairs={{0,4},{4,8},{8,12},{12,0},{1,5},{5,9},{9,13},{13,1},{2,6},{6,10},{... | collective-permute-start | bytes 15728648 | tf_op jit(solution)/shard_map/ppermute | solution.py:25
  4113.4 8.3 broadcast_in_dim.86
  4121.7 5.8 constant_dynamic-update-slice_fusion.4
  4127.4 5.8 constant_dynamic-update-slice_fusion.3
  4133.2 6.0 constant_dynamic-update-slice_fusion.2
  4139.2 87.3 %collective-permute-done.2 = bf16[1280,2048]{1,0:T(8,128)(2,1)} collective-permute-done((bf16[1280,2048]{1,0:T(8,128)(2,1)}, bf16[1280,2048]{1,0:T(8,128)(2,1)}, u32[]{:S(2)}, u32[]{:S(2)}) %collective-permute-start.2) | collective-permute-done | bytes 5242912 | tf_op jit(solution)/shard_map/ppermute | solution.py:25
  4226.5 5.7 constant_dynamic-update-slice_fusion.1
  4232.4 11.6 fusion.31
  4244.2 6.6 fusion.44
  4250.9 16.9 all-reduce.9
  4268.1 13.3 all-reduce.7
  4281.4 1.3 fusion.43
  4282.8 54.2 %all-reduce.13.cloned.1.call-done = (f32[512,1920]{1,0:T(8,128)}, f32[320,2048]{1,0:T(8,128)}, f32[512,10240]{1,0:T(8,128)}, f32[1280,2048]{1,0:T(8,128)}) async-done(((f32[512,1920]{1,0:T(8,128)}, f32[320,2048]{1,0:T(8,128)}, f32[512,10240]{1,0:T(8,128)}, f32[1280,2048]{1,0:T(8,128)}), (f32[512,1920]{1,0:T(8,128)}, f32[320,2048]{1,0:T(8,128)}, f32[512,10240]{1,0:T(8,128)}, ...) | async-done | bytes 38010896 | tf_op jit(solution)/shard_map/psum | solution.py:348
  4337.0 4.4 copy.201
  4341.4 1.5 copy.202
  4342.9 18.0 copy.203
  4360.9 4.1 copy.204
  (223 shorter events, 34.1 us)
Async XLA Ops:
  7.2 146.6 %all-gather.7.cloned.1.call-start = ((), (), s32[]{:S(2)}) async-start(), calls=%async_computation.5 | async-start | bytes 9830400 | tf_op jit(solution)/shard_map/all_gather | solution.py:129
  7.9 243.8 %all-gather.9.cloned.1.call-start = ((), (), s32[]{:S(2)}) async-start(), calls=%async_computation.6 | async-start | bytes 6553600 | tf_op jit(solution)/shard_map/all_gather | solution.py:132
  8.7 942.8 %all-gather.11.cloned.1.call-start = ((), (), s32[]{:S(2)}) async-start(), calls=%async_computation.7 | async-start | bytes 52428800 | tf_op jit(solution)/shard_map/all_gather | solution.py:218
  9.4 15.0 copy-start.35
  9.4 16.2 copy-start.42
  9.4 16.5 copy-start.43
  9.4 29.7 copy-start.37
  9.4 42.9 copy-start
  9.5 1298.5 %all-gather.13.cloned.1.call-start = ((), (), s32[]{:S(2)}) async-start(), calls=%async_computation.8 | async-start | bytes 26214400 | tf_op jit(solution)/shard_map/all_gather | solution.py:234
  10.0 1366.4 %reduce-scatter.8.cloned.1.call-start = ((), (), s32[]{:S(2)}) async-start(), calls=%async_computation.9 | async-start | bytes 983040 | tf_op jit(solution)/shard_map/reduce_scatter | solution.py:310
  39.1 119.2 %copy-start.38 = (bf16[64]{0:T(256)(128)(2,1)}, bf16[64]{0:T(256)(128)(2,1)S(1)}, u32[]{:S(2)}) copy-start(bf16[64]{0:T(256)(128)(2,1)S(1)} %get-tuple-element.448) | copy-start | bytes 388
  39.1 119.2 %copy-start.40 = (bf16[64]{0:T(256)(128)(2,1)}, bf16[64]{0:T(256)(128)(2,1)S(1)}, u32[]{:S(2)}) copy-start(bf16[64]{0:T(256)(128)(2,1)S(1)} %get-tuple-element.449) | copy-start | bytes 388
  39.1 119.6 %copy-start.31 = (f32[64]{0:T(128)}, f32[64]{0:T(128)S(1)}, u32[]{:S(2)}) copy-start(f32[64]{0:T(128)S(1)} %convert_element_type.96) | copy-start | bytes 772
  39.1 128.0 %copy-start.33 = (f32[64]{0:T(128)}, f32[64]{0:T(128)S(1)}, u32[]{:S(2)}) copy-start(f32[64]{0:T(128)S(1)} %convert_element_type.99) | copy-start | bytes 772
  52.3 1289.8 %copy-start.29 = (f32[128]{0:T(128)}, f32[128]{0:T(128)S(1)}, u32[]{:S(2)}) copy-start(f32[128]{0:T(128)S(1)} %compare_convert_fusion) | copy-start | bytes 1540
  52.5 105.8 %copy-start.26 = (f32[128]{0:T(128)}, f32[128]{0:T(128)S(1)}, u32[]{:S(2)}) copy-start(f32[128]{0:T(128)S(1)} %add_rsqrt_fusion.3) | copy-start | bytes 1540
  52.7 114.6 %copy-start.14 = (f32[128,32]{0,1:T(8,128)}, f32[128,32]{0,1:T(8,128)S(1)}, u32[]{:S(2)}) copy-start(f32[128,32]{0,1:T(8,128)S(1)} %get-tuple-element.481) | copy-start | bytes 49156
  52.7 114.6 %copy-start.16 = (f32[128,32]{0,1:T(8,128)}, f32[128,32]{0,1:T(8,128)S(1)}, u32[]{:S(2)}) copy-start(f32[128,32]{0,1:T(8,128)S(1)} %get-tuple-element.482) | copy-start | bytes 49156
  158.3 7.6 copy-start.6
  158.6 8.7 copy-start.9
  158.7 8.7 copy-start.20
  175.5 79.7 %copy-start.11 = (bf16[128,5,4,64]{0,3,2,1:T(8,128)(2,1)}, bf16[128,5,4,64]{0,3,2,1:T(8,128)(2,1)S(1)}, u32[]{:S(2)}) copy-start(bf16[128,5,4,64]{0,3,2,1:T(8,128)(2,1)S(1)} %convert_element_type.100) | copy-start | bytes 983044
  255.2 1086.9 %copy-start.22 = (f32[128]{0:T(128)}, f32[128]{0:T(128)S(1)}, u32[]{:S(2)}) copy-start(f32[128]{0:T(128)S(1)} %add_rsqrt_fusion.2) | copy-start | bytes 1540
  951.5 356.5 %copy-start.13 = (bf16[1,128,2048]{2,1,0:T(8,128)(2,1)S(1)}, bf16[1,128,2048]{2,1,0:T(8,128)(2,1)}, u32[]{:S(2)}) copy-start(bf16[1,128,2048]{2,1,0:T(8,128)(2,1)} %param.18) | copy-start | bytes 1572868
  1355.8 201.6 %reduce-scatter.12.cloned.1.call-start = ((), (), s32[]{:S(2)}) async-start(), calls=%async_computation.11 | async-start | bytes 13107200 | tf_op jit(solution)/shard_map/reduce_scatter | solution.py:346
  1362.8 5.2 copy-start.15
  1362.9 5.2 copy-start.17
  1362.9 5.3 copy-start.4
  1362.9 5.3 copy-start.34
  1362.9 461.3 %reduce-scatter.10.cloned.1.call-start = ((), (), s32[]{:S(2)}) async-start(), calls=%async_computation.10 | async-start | bytes 19660800 | tf_op jit(solution)/shard_map/reduce_scatter | solution.py:343
  1371.5 6.8 copy-start.10
  1372.6 5.7 copy-start.21
  1372.6 5.7 copy-start.32
  1372.6 5.9 copy-start.28
  1372.6 7.3 copy-start.27
  1379.9 8.5 copy-start.8
  1388.4 1125.6 %reduce-scatter.14.cloned.1.call-start = ((), (), s32[]{:S(2)}) async-start(), calls=%async_computation.12 | async-start | bytes 52428800 | tf_op jit(solution)/shard_map/reduce_scatter | solution.py:252
  1407.2 2475.3 %reduce-scatter.16.cloned.1.call-start = ((), (), s32[]{:S(2)}) async-start(), calls=%async_computation.13 | async-start | bytes 104857600
  1438.7 2898.2 %all-reduce.13.cloned.1.call-start = ((), (), s32[]{:S(2)}) async-start(), calls=%async_computation.14 | async-start | bytes 76021760 | tf_op jit(solution)/shard_map/psum | solution.py:348
  3882.6 118.1 %collective-permute-start = (bf16[1280,2048]{1,0:T(8,128)(2,1)}, bf16[1280,2048]{1,0:T(8,128)(2,1)}, u32[]{:S(2)}, u32[]{:S(2)}) collective-permute-start(bf16[1280,2048]{1,0:T(8,128)(2,1)} %param.27), channel_id=1, source_target_pairs={{0,4},{4,8},{8,12},{12,0},{1,5},{5,9},{9,13},{13,1},{2,6},{6,10},{... | collective-permute-start | bytes 15728648 | tf_op jit(solution)/shard_map/ppermute | solution.py:25
  3882.6 250.6 %collective-permute-start.1 = (bf16[1280,2048]{1,0:T(8,128)(2,1)}, bf16[1280,2048]{1,0:T(8,128)(2,1)}, u32[]{:S(2)}, u32[]{:S(2)}) collective-permute-start(bf16[1280,2048]{1,0:T(8,128)(2,1)} %param.27), channel_id=1, source_target_pairs={{0,12},{4,0},{8,4},{12,8},{1,13},{5,1},{9,5},{13,9},{2,14},{6,2},{... | collective-permute-start | bytes 15728648 | tf_op jit(solution)/shard_map/ppermute | solution.py:32
  4000.7 225.9 %collective-permute-start.2 = (bf16[1280,2048]{1,0:T(8,128)(2,1)}, bf16[1280,2048]{1,0:T(8,128)(2,1)}, u32[]{:S(2)}, u32[]{:S(2)}) collective-permute-start(bf16[1280,2048]{1,0:T(8,128)(2,1)} %collective-permute-done), channel_id=1, source_target_pairs={{0,4},{4,8},{8,12},{12,0},{1,5},{5,9},{9,13},{13,1},{2,6},{6,10},{... | collective-permute-start | bytes 15728648 | tf_op jit(solution)/shard_map/ppermute | solution.py:25
  4244.2 6.6 copy-start.24
  4244.2 37.2 copy-start.2
  4337.0 4.4 copy-start.12
  4341.4 19.5 slice-start
  4342.9 18.0 slice-start.1
  4342.9 18.0 slice-start.2
  (12 other events, 17.9 us)
Sparse Core Ops, SparseCore 0:
  9.6 144.1 all-gather.6
  155.3 96.3 all-gather.8
  253.3 698.1 all-gather.10
  952.9 355.0 all-gather.12
  1356.0 20.4 reduce-scatter.7
  1379.4 177.9 reduce-scatter.11
  1560.5 263.6 reduce-scatter.9
  1826.7 687.3 reduce-scatter.13
  2516.4 1366.0 reduce-scatter.15
  3887.2 449.7 all-reduce.12
